TPU v7x, 32 devices: a whole 2x2x4 slice. The times are simulated.
32 devices in a mesh: dp: 16 (over z, y, core), head: 2 (over x).
Axes of the slice: x: 2, y: 2, z: 4, core: 2. Of those that a mesh axis runs over, the one named last changes fastest.
Arguments:
- tokens: bfloat16 [2, 16384, 768], P(None, ('dp', 'head')), may hold values from -6 to 6
- segment_ids: int32 [2, 32, 512], P(None, 'dp'), may hold values from 0 to 15, never falling along the last dimension, each value on 1 to 256 neighbouring positions
- w_qkv: bfloat16 [3, 768, 768], P(None, 'dp', 'head'), may hold values from -0.21875 to 0.21875
- qv_bias: float32 [2, 768], replicated, may hold values from -3 to 3
- w_out: bfloat16 [768, 768], P(None, ('dp', 'head')), may hold values from -0.875 to 0.875
- out_bias: float32 [768], replicated, may hold values from -3 to 3
- w_in: bfloat16 [768, 3072], P(None, ('dp', 'head')), may hold values from -0.21875 to 0.21875
- in_bias: float32 [3072], replicated, may hold values from -3 to 3
- w_back: bfloat16 [3072, 768], P(None, ('dp', 'head')), may hold values from -0.109375 to 0.109375
- back_bias: float32 [768], replicated, may hold values from -3 to 3
- norm_gains: float32 [2, 768], replicated, may hold values from 0.25 to 1.75
- norm_shifts: float32 [2, 768], replicated, may hold values from -2 to 2
- out_cotangent: bfloat16 [2, 16384, 768], P(None, ('dp', 'head')), may hold values from -6 to 6
Outputs:
- out: bfloat16 [2, 16384, 768], P(None, ('dp', 'head'))
- x_grad: float32 [2, 16384, 768], P(None, ('dp', 'head'))
- w_qkv_grad: float32 [3, 768, 768], P(None, 'dp', 'head')
- qv_bias_grad: float32 [2, 768], replicated
- w_out_grad: float32 [768, 768], P(None, ('dp', 'head'))
- out_bias_grad: float32 [768], replicated
- w_in_grad: float32 [768, 3072], P(None, ('dp', 'head'))
- in_bias_grad: float32 [3072], replicated
- w_back_grad: float32 [3072, 768], P(None, ('dp', 'head'))
- back_bias_grad: float32 [768], replicated
- norm_gains_grad: float32 [2, 768], replicated
- norm_shifts_grad: float32 [2, 768], replicated
Inputs may be any that keep to these rules, and one draw needn't show every extreme that they name: `segment_ids`: within each packed row of 512 positions the ids never fall; a run of one id is at most 256 positions and one run in each row has that length.
All inputs are finite; a program needn't handle non-finite values.
Results may differ from a plain program's by a relative error of at most 0.014.
The roundings to bfloat16 on the way count: a program that leaves them out, or rounds other values in their place, can miss the bound.
Values may be sent and summed in bfloat16 or wider, within the bound.
A program may use at most 192 MiB of HBM per device.

v0:
```python
import jax
import jax.numpy as jnp
from jax import lax
from jax.sharding import PartitionSpec as P

HD = 64
NORM_EPS = 1e-05
MASKED = -1e30


def layer_norm(residual, norm_gain, offset):
    average = jnp.mean(residual, axis=-1, keepdims=True)
    centred = residual - average
    spread = jnp.mean(centred * centred, axis=-1, keepdims=True)
    return centred * lax.rsqrt(spread + NORM_EPS) * norm_gain + offset


def exact_gelu(inputs):
    return jax.nn.gelu(inputs, approximate=False)


def scores_of(queries, key_rows, segment):
    raw_scores = jnp.einsum("qhd,khd->hqk", queries, key_rows, preferred_element_type=jnp.float32)
    same_doc = segment[:, None] == segment[None, :]
    return jnp.where(same_doc[None], raw_scores * HD ** (-0.5), MASKED)


def attend_forward(block_items):
    queries, key_rows, values, segment = block_items
    scores = scores_of(queries, key_rows, segment)
    highest = jnp.max(scores, axis=-1, keepdims=True)
    exponent = jnp.exp(scores - highest)
    totals = jnp.sum(exponent, axis=-1, keepdims=True)
    probabilities = (exponent / totals).astype(jnp.bfloat16)
    context = jnp.einsum("hqk,khd->qhd", probabilities, values, preferred_element_type=jnp.float32)
    return (context.astype(jnp.bfloat16), highest[..., 0] + jnp.log(totals[..., 0]))


def attend_backward(block_items):
    queries, key_rows, values, segment, log_total, grad_context = block_items
    scores = scores_of(queries, key_rows, segment)
    probabilities = jnp.exp(scores - log_total[..., None])
    grad_probs = jnp.einsum(
        "qhd,khd->hqk", grad_context, values, preferred_element_type=jnp.float32
    )
    grad_values = jnp.einsum(
        "hqk,qhd->khd",
        probabilities.astype(jnp.bfloat16),
        grad_context,
        preferred_element_type=jnp.float32,
    )
    weighted = jnp.sum(probabilities * grad_probs, axis=-1, keepdims=True)
    grad_scores = (probabilities * (grad_probs - weighted)).astype(jnp.bfloat16)
    scale = HD ** (-0.5)
    grad_queries = (
        jnp.einsum("hqk,khd->qhd", grad_scores, key_rows, preferred_element_type=jnp.float32)
        * scale
    )
    grad_keys = (
        jnp.einsum("hqk,qhd->khd", grad_scores, queries, preferred_element_type=jnp.float32) * scale
    )
    return (
        grad_queries.astype(jnp.bfloat16),
        grad_keys.astype(jnp.bfloat16),
        grad_values.astype(jnp.bfloat16),
    )


def fetch_weights(w_qkv, w_out, w_in, w_back):
    head_full = lax.all_gather(w_qkv, "dp", axis=1, tiled=True)
    out_full, in_full, back_full = (
        lax.all_gather(w_out, ("dp", "head"), axis=1, tiled=True),
        lax.all_gather(w_in, ("dp", "head"), axis=1, tiled=True),
        lax.all_gather(w_back, ("dp", "head"), axis=1, tiled=True),
    )
    return (head_full, out_full, in_full, back_full)


def reduce_heads(head_term):
    return lax.psum_scatter(head_term, "dp", scatter_dimension=1, tiled=True)


def reduce_tokens(token_terms):
    return (
        lax.psum_scatter(token_terms[0], ("dp", "head"), scatter_dimension=1, tiled=True),
        lax.psum_scatter(token_terms[1], ("dp", "head"), scatter_dimension=1, tiled=True),
        lax.psum_scatter(token_terms[2], ("dp", "head"), scatter_dimension=1, tiled=True),
    )


def accumulate(total, term):
    if total is None:
        return term
    return jax.tree.map(jnp.add, total, term)


def on_device(
    tokens,
    segment_ids,
    w_qkv,
    qv_bias,
    w_out,
    out_bias,
    w_in,
    in_bias,
    w_back,
    back_bias,
    norm_gains,
    norm_shifts,
    out_cotangent,
):
    micro_count = tokens.shape[0]
    head_width = w_qkv.shape[2]
    head_count = head_width // HD
    seq_count = segment_ids.shape[1]
    seq_len = segment_ids.shape[2]
    head_start = lax.axis_index("head") * head_width
    bias_local = lax.dynamic_slice_in_dim(qv_bias, head_start, head_width, 1)
    head_shape = (seq_count, seq_len, head_count, HD)
    fetched = None
    head_total = None
    token_total = None
    small_total = None
    outputs = []
    input_grads = []
    for micro_idx in range(micro_count):
        fetched = fetch_weights(w_qkv, w_out, w_in, w_back)
        head_full, out_full, in_full, back_full = fetched
        x_local = tokens[micro_idx]
        x_group = lax.all_gather(x_local, "head", axis=0, tiled=True)
        projected = jnp.einsum(
            "td,cdf->ctf", x_group, head_full, preferred_element_type=jnp.float32
        )
        queries = (projected[0] + bias_local[0]).astype(jnp.bfloat16).reshape(head_shape)
        key_rows = projected[1].astype(jnp.bfloat16).reshape(head_shape)
        values = (projected[2] + bias_local[1]).astype(jnp.bfloat16).reshape(head_shape)
        segments = segment_ids[micro_idx]
        context, log_total = lax.map(attend_forward, (queries, key_rows, values, segments))
        context = context.reshape(seq_count * seq_len, head_width)
        ctx_tokens = lax.all_to_all(context, "head", split_axis=0, concat_axis=1, tiled=True)
        attended = jnp.dot(ctx_tokens, out_full, preferred_element_type=jnp.float32) + out_bias
        resid_one = x_local.astype(jnp.float32) + attended
        hidden, norm_first = jax.vjp(layer_norm, resid_one, norm_gains[0], norm_shifts[0])
        hidden_low = hidden.astype(jnp.bfloat16)
        pre_act = jnp.dot(hidden_low, in_full, preferred_element_type=jnp.float32) + in_bias
        activation, gelu_back = jax.vjp(exact_gelu, pre_act)
        activation_low = activation.astype(jnp.bfloat16)
        branch = jnp.dot(activation_low, back_full, preferred_element_type=jnp.float32) + back_bias
        result, norm_second = jax.vjp(layer_norm, hidden + branch, norm_gains[1], norm_shifts[1])
        outputs.append(result.astype(jnp.bfloat16))
        grad_two, gain_two, shift_two = norm_second(out_cotangent[micro_idx].astype(jnp.float32))
        grad_branch = grad_two.astype(jnp.bfloat16)
        back_term = jnp.einsum(
            "tf,td->fd", activation_low, grad_branch, preferred_element_type=jnp.float32
        )
        grad_act = jnp.einsum(
            "td,fd->tf", grad_branch, back_full, preferred_element_type=jnp.float32
        )
        grad_pre = gelu_back(grad_act)[0].astype(jnp.bfloat16)
        in_term = jnp.einsum("td,tf->df", hidden_low, grad_pre, preferred_element_type=jnp.float32)
        grad_hidden = grad_two + jnp.einsum(
            "tf,df->td", grad_pre, in_full, preferred_element_type=jnp.float32
        )
        grad_one, gain_one, shift_one = norm_first(grad_hidden)
        grad_attn = grad_one.astype(jnp.bfloat16)
        out_term = jnp.einsum(
            "tc,td->cd", ctx_tokens, grad_attn, preferred_element_type=jnp.float32
        )
        grad_ctx = jnp.einsum(
            "td,cd->tc", grad_attn, out_full, preferred_element_type=jnp.float32
        ).astype(jnp.bfloat16)
        grad_heads = lax.all_to_all(grad_ctx, "head", split_axis=1, concat_axis=0, tiled=True)
        grad_queries, grad_keys, grad_values = lax.map(
            attend_backward,
            (queries, key_rows, values, segments, log_total, grad_heads.reshape(head_shape)),
        )
        grad_proj = jnp.stack(
            [
                grad_queries.reshape(-1, head_width),
                grad_keys.reshape(-1, head_width),
                grad_values.reshape(-1, head_width),
            ]
        )
        head_term = jnp.einsum(
            "td,ctf->cdf", x_group, grad_proj, preferred_element_type=jnp.float32
        )
        grad_input = lax.psum_scatter(
            jnp.einsum(
                "ctf,cdf->td", grad_proj, head_full, preferred_element_type=jnp.float32
            ).astype(jnp.bfloat16),
            "head",
            scatter_dimension=0,
            tiled=True,
        ).astype(jnp.float32)
        input_grads.append(grad_one + grad_input)
        bias_heads = jnp.stack(
            [
                jnp.sum(grad_proj[0].astype(jnp.float32), axis=0),
                jnp.sum(grad_proj[2].astype(jnp.float32), axis=0),
            ]
        )
        bias_full = lax.dynamic_update_slice(
            jnp.zeros(qv_bias.shape, jnp.float32),
            bias_heads,
            (jnp.zeros((), jnp.int32), head_start),
        )
        small_term = (
            bias_full,
            jnp.sum(grad_attn.astype(jnp.float32), axis=0),
            jnp.sum(grad_pre.astype(jnp.float32), axis=0),
            jnp.sum(grad_branch.astype(jnp.float32), axis=0),
            jnp.stack([gain_one, gain_two]),
            jnp.stack([shift_one, shift_two]),
        )
        small_total = accumulate(small_total, small_term)
        token_term = (out_term, in_term, back_term)
        head_total = accumulate(head_total, reduce_heads(head_term))
        token_total = accumulate(token_total, reduce_tokens(token_term))
    small_sums = lax.psum(
        (
            small_total[0],
            small_total[1],
            small_total[2],
            small_total[3],
            small_total[4],
            small_total[5],
        ),
        ("dp", "head"),
    )
    return (
        jnp.stack(outputs),
        jnp.stack(input_grads),
        head_total,
        small_sums[0],
        token_total[0],
        small_sums[1],
        token_total[1],
        small_sums[2],
        token_total[2],
        small_sums[3],
        small_sums[4],
        small_sums[5],
    )


def solution(mesh):
    return jax.shard_map(
        on_device,
        mesh=mesh,
        in_specs=(
            P(None, ("dp", "head"), None),
            P(None, "dp", None),
            P(None, "dp", "head"),
            P(),
            P(None, ("dp", "head")),
            P(),
            P(None, ("dp", "head")),
            P(),
            P(None, ("dp", "head")),
            P(),
            P(),
            P(),
            P(None, ("dp", "head"), None),
        ),
        out_specs=(
            P(None, ("dp", "head"), None),
            P(None, ("dp", "head"), None),
            P(None, "dp", "head"),
            P(),
            P(None, ("dp", "head")),
            P(),
            P(None, ("dp", "head")),
            P(),
            P(None, ("dp", "head")),
            P(),
            P(),
            P(),
        ),
        check_vma=False,
    )
```

profile of v0, /device:TPU:0, one launch (start us, length us, event | category | flops | bytes accessed | tf_op | source)
XLA Modules:
  0.0 1031.0 jit_solution(9810883486489578737)
XLA Ops:
  14.0 26.0 %all-gather.19.cloned.1.call-done = bf16[1,1024,768]{2,1,0:T(8,128)(2,1)} async-done(((bf16[1,512,768]{2,1,0:T(8,128)(2,1)}), bf16[1,1024,768]{2,1,0:T(8,128)(2,1)}) %all-gather.19.cloned.1.call-update) | async-done | bytes 1572880 | tf_op jit(solution)/shard_map/all_gather | solution.py:130
  40.1 42.8 %all-gather.9.cloned.1.call-done = bf16[3,768,384]{2,1,0:T(8,128)(2,1)} async-done(((bf16[3,48,384]{2,1,0:T(8,128)(2,1)}), bf16[3,768,384]{2,1,0:T(8,128)(2,1)}) %all-gather.9.cloned.1.call-update) | async-done | bytes 1769488 | tf_op jit(solution)/shard_map/all_gather | solution.py:70
  82.9 4.0 convolution_bitcast_fusion
  88.1 22.8 %all-gather.17.cloned.1.call-done = bf16[1,1024,768]{2,1,0:T(8,128)(2,1)} async-done(((bf16[1,512,768]{2,1,0:T(8,128)(2,1)}), bf16[1,1024,768]{2,1,0:T(8,128)(2,1)}) %all-gather.17.cloned.1.call-update) | async-done | bytes 1572880 | tf_op jit(solution)/shard_map/all_gather | solution.py:130
  110.9 4.0 convolution_bitcast_fusion.1
  117.8 3.7 squeeze.80
  121.5 3.4 squeeze.82
  130.5 4.8 fusion.149
  136.3 11.5 %while.53 = (s32[]{:T(128)}, bf16[2,512,6,64]{1,3,2,0:T(8,128)(2,1)}, f32[2,6,512]{2,1,0:T(8,128)S(1)}, bf16[2,512,6,64]{1,3,2,0:T(8,128)(2,1)S(1)}, s32[2,512]{...) while((s32[]{:T(128)}, ...), condition=%wide.region_11.12_spmd, body=%wide.region_8.11_spmd.sunk | while | flops 421983232 | bytes 21622876 | solution.py:138
  147.8 4.3 all-to-all-start.1
  152.1 3.3 convert_element_type.201
  157.6 11.3 %while.52 = (s32[]{:T(128)}, bf16[2,512,6,64]{1,3,2,0:T(8,128)(2,1)}, f32[2,6,512]{2,1,0:T(8,128)S(1)}, bf16[2,512,6,64]{1,3,2,0:T(8,128)(2,1)}, s32[2,512]{1,0:...) while((s32[]{:T(128)}, ...), condition=%wide.region_3.4_spmd, body=%wide.region_0.3_spmd.sunk | while | flops 421983232 | bytes 31060144 | solution.py:138
  168.9 3.5 all-to-all-start
  172.5 3.7 fusion.181
  176.3 8.2 all-to-all-done
  188.7 46.1 %all-gather.13.cloned.1.call-done = bf16[768,3072]{0,1:T(8,128)(2,1)} async-done(((bf16[768,96]{0,1:T(8,128)(2,1)}), bf16[768,3072]{0,1:T(8,128)(2,1)}) %all-gather.13.cloned.1.call-update) | async-done | bytes 4718608 | tf_op jit(solution)/shard_map/all_gather | solution.py:73
  234.8 5.3 fusion.165
  242.7 35.5 %multiply_convert_fusion.3 = (bf16[512,3072]{1,0:T(8,128)(2,1)}, f32[512,3072]{1,0:T(8,128)}, bf16[512,3072]{1,0:T(8,128)(2,1)}, f32[512,3072]{1,0:T(8,128)}, f32[512,3072]{1,0:T(8,128)}) fusion(f32[3072]{0:T(1024)S(1)} %copy-done.108, f32[512,3072]{1,0:T(8,128)S(1)} %fusion.165, bf16[768,3072]{0,1:T(8,128)(2,1)S(1)} %copy-done.104, ...), kind=kOutput, calls=%fused_computation.153 | convolution fusion | flops 2625503232 | bytes 37771264 | tf_op jit(solution)/shard_map/dot_general | solution.py:145
  278.2 21.2 %all-gather.15.cloned.1.call-done = bf16[3072,768]{0,1:T(8,128)(2,1)} async-done(((bf16[3072,24]{0,1:T(8,128)(2,1)}), bf16[3072,768]{0,1:T(8,128)(2,1)}) %all-gather.15.cloned.1.call-update) | async-done | bytes 4718608 | tf_op jit(solution)/shard_map/all_gather | solution.py:74
  299.5 6.2 fusion.183
  306.1 2.8 fusion.182
  311.1 2.7 fusion.174
  319.2 17.3 %convert_reduce_fusion.1 = (f32[3072]{0:T(1024)}, bf16[512,3072]{1,0:T(8,128)(2,1)}, f32[3072]{0:T(1024)}, bf16[512,3072]{1,0:T(8,128)(2,1)}) fusion(f32[512,3072]{1,0:T(8,128)} %get-tuple-element.505, f32[512,3072]{1,0:T(8,128)} %get-tuple-element.546, f32[3072]{0:T(1024)S(1)} %copy-done.108, f32[512,3072]{1,0:T(8,128)S(1)} %fusion.184, ...), kind=kOutput, calls=%fused_computation.137 | convolution fusion | flops 2469390336 | bytes 43290624 | tf_op jit(solution)/shard_map/td,fd->tf/dot_general | solution.py:156
  336.5 6.5 add_add_fusion.6
  343.0 6.2 multiply_reduce_fusion.3
  349.3 2.8 fusion.171
  356.1 4.3 all-to-all-start.2
  363.1 8.9 all-to-all-done.2
  372.0 4.3 all-to-all-start.3
  381.6 22.9 %while.54 = (s32[]{:T(128)}, bf16[2,512,6,64]{1,3,2,0:T(8,128)(2,1)}, bf16[2,512,6,64]{1,3,2,0:T(8,128)(2,1)}, bf16[2,512,6,64]{1,3,2,0:T(8,128)(2,1)}, bf16[2,5...) while((s32[]{:T(128)}, ...), condition=%wide.region_22.23_spmd, body=%wide.region_20.22_spmd.sunk | while | flops 1031468032 | bytes 68001024 | solution.py:173
  409.9 23.3 %while.55 = (s32[]{:T(128)}, bf16[2,512,6,64]{1,3,2,0:T(8,128)(2,1)}, bf16[2,512,6,64]{1,3,2,0:T(8,128)(2,1)}, bf16[2,512,6,64]{1,3,2,0:T(8,128)(2,1)}, bf16[2,5...) while((s32[]{:T(128)}, ...), condition=%wide.region_30.31_spmd, body=%wide.region_28.30_spmd.sunk | while | flops 1031468032 | bytes 68001024 | solution.py:173
  451.4 4.4 fusion.144
  458.1 4.0 copy.155
  463.7 4.9 bitcast_convert_fusion.1
  468.6 5.5 bitcast_convert_fusion
  475.3 3.5 convolution_add_fusion.2
  478.9 4.8 fusion.186
  483.8 5.5 convolution_add_fusion
  490.7 4.9 fusion.167
  495.6 5.4 convolution_add_fusion.1
  504.2 2.9 pad_maximum_fusion.3
  511.7 42.3 %all-reduce.1 = (f32[2,768]{1,0:T(2,128)}, f32[768]{0:T(1024)}, f32[3072]{0:T(1024)}, f32[768]{0:T(1024)}, f32[2,768]{1,0:T(2,128)}, /*index=5*/f32[2,768]{1,0:T(2,128)}) all-reduce(f32[2,768]{1,0:T(2,128)S(1)} %fusion.155, f32[768]{0:T(1024)S(1)} %add.321, f32[3072]{0:T(1024)S(1)} %add.323, ...), channel_id=1, replica_groups=mesh['dp'=16,'head'=2] {'dp','head'}, use_global_device_ids=true, to_apply=%region_38.39 | all-reduce | flops 9216 | bytes 73728 | tf_op jit(solution)/shard_map/psum | solution.py:219
  554.1 25.0 %all-reduce.4.cloned.1.call-done = f32[3,768,384]{2,0,1:T(4,128)} async-done(((f32[3,768,384]{2,0,1:T(4,128)}), f32[3,768,384]{2,0,1:T(4,128)}) %all-reduce.4.cloned.1.call-update) | async-done | bytes 3538960
  580.8 26.1 %reduce-scatter.6.cloned.1.call-done = bf16[512,768]{1,0:T(8,128)(2,1)} async-done(((bf16[1024,768]{1,0:T(8,128)(2,1)}), bf16[512,768]{1,0:T(8,128)(2,1)}) %reduce-scatter.6.cloned.1.call-update) | async-done | bytes 786448 | tf_op jit(solution)/shard_map/reduce_scatter | solution.py:187
  609.4 26.0 %reduce-scatter.8.cloned.1.call-done = bf16[512,768]{1,0:T(8,128)(2,1)} async-done(((bf16[1024,768]{1,0:T(8,128)(2,1)}), bf16[512,768]{1,0:T(8,128)(2,1)}) %reduce-scatter.8.cloned.1.call-update) | async-done | bytes 786448 | tf_op jit(solution)/shard_map/reduce_scatter | solution.py:187
  638.7 102.0 %reduce-scatter.10.cloned.1.call-done = f32[768,24]{0,1:T(8,128)} async-done(((f32[768,768]{0,1:T(8,128)}), f32[768,24]{0,1:T(8,128)}) %reduce-scatter.10.cloned.1.call-update) | async-done | bytes 73744 | tf_op jit(solution)/shard_map/reduce_scatter | solution.py:85
  740.8 141.7 %reduce-scatter.14.cloned.1.call-done = f32[3072,24]{0,1:T(8,128)} async-done(((f32[3072,768]{0,1:T(8,128)}), f32[3072,24]{0,1:T(8,128)}) %reduce-scatter.14.cloned.1.call-update) | async-done | bytes 294928 | tf_op jit(solution)/shard_map/reduce_scatter | solution.py:87
  882.4 141.5 %reduce-scatter.12.cloned.1.call-done = f32[768,96]{0,1:T(8,128)} async-done(((f32[768,3072]{0,1:T(8,128)}), f32[768,96]{0,1:T(8,128)}) %reduce-scatter.12.cloned.1.call-update) | async-done | bytes 294928 | tf_op jit(solution)/shard_map/reduce_scatter | solution.py:86
  (452 shorter events, 158.0 us)
Async XLA Ops:
  7.2 32.9 %all-gather.19.cloned.1.call-start = ((), (), s32[]{:S(2)}) async-start(), calls=%async_computation.16 | async-start | bytes 2359296 | tf_op jit(solution)/shard_map/all_gather | solution.py:130
  9.9 73.0 %all-gather.9.cloned.1.call-start = ((), (), s32[]{:S(2)}) async-start(), calls=%async_computation.9 | async-start | bytes 1880064 | tf_op jit(solution)/shard_map/all_gather | solution.py:70
  10.7 100.2 %all-gather.17.cloned.1.call-start = ((), (), s32[]{:S(2)}) async-start(), calls=%async_computation.15 | async-start | bytes 2359296 | tf_op jit(solution)/shard_map/all_gather | solution.py:130
  11.4 161.1 %all-gather.11.cloned.1.call-start = ((), (), s32[]{:S(2)}) async-start(), calls=%async_computation.10 | async-start | bytes 1216512 | tf_op jit(solution)/shard_map/all_gather | solution.py:72
  12.0 222.8 %all-gather.13.cloned.1.call-start = ((), (), s32[]{:S(2)}) async-start(), calls=%async_computation.11 | async-start | bytes 4866048 | tf_op jit(solution)/shard_map/all_gather | solution.py:73
  12.6 286.9 %all-gather.15.cloned.1.call-start = ((), (), s32[]{:S(2)}) async-start(), calls=%async_computation.12 | async-start | bytes 4866048 | tf_op jit(solution)/shard_map/all_gather | solution.py:74
  14.0 292.0 %copy-start.72 = (f32[768]{0:T(1024)}, f32[768]{0:T(1024)S(1)}, u32[]{:S(2)}) copy-start(f32[768]{0:T(1024)S(1)} %get-tuple-element.407) | copy-start | bytes 9220
  14.0 335.3 %copy-start.70 = (f32[768]{0:T(1024)}, f32[768]{0:T(1024)S(1)}, u32[]{:S(2)}) copy-start(f32[768]{0:T(1024)S(1)} %get-tuple-element.554) | copy-start | bytes 9220
  147.7 8.9 copy-start.66
  147.7 9.8 copy-start
  147.7 9.8 copy-start.62
  147.7 9.8 copy-start.20
  147.8 21.2 %all-to-all-start.1 = ((bf16[2,512,384]{1,2,0:T(8,128)(2,1)}), bf16[2,512,384]{1,2,0:T(8,128)(2,1)}, u32[]{:S(2)}, u32[]{:S(2)}) async-start(bf16[2,512,384]{1,2,0:T(8,128)(2,1)} %bitcast.52), calls=%async_computation.1 | async-start | bytes 1572864 | tf_op jit(solution)/shard_map/all_to_all | solution.py:140
  157.6 15.0 %copy-start.109 = (f32[768]{0:T(1024)S(1)}, f32[768]{0:T(1024)}, u32[]{:S(2)}) copy-start(f32[768]{0:T(1024)} %param.26) | copy-start | bytes 9220
  168.9 7.3 copy-start.2
  168.9 7.3 copy-start.6
  168.9 7.3 copy-start.64
  168.9 7.3 copy-start.68
  168.9 15.5 %all-to-all-start = ((bf16[2,512,384]{1,2,0:T(8,128)(2,1)}), bf16[2,512,384]{1,2,0:T(8,128)(2,1)S(1)}, u32[]{:S(2)}, u32[]{:S(2)}) async-start(bf16[2,512,384]{1,2,0:T(8,128)(2,1)} %bitcast.373), calls=%async_computation | async-start | bytes 1572864 | tf_op jit(solution)/shard_map/all_to_all | solution.py:140
  176.3 11.7 %copy-start.14 = (f32[512,768]{1,0:T(8,128)S(1)}, f32[512,768]{1,0:T(8,128)}, u32[]{:S(2)}) copy-start(f32[512,768]{1,0:T(8,128)} %get-tuple-element.545) | copy-start | bytes 4718596
  176.3 173.0 %copy-start.74 = (f32[512]{0:T(512)}, f32[512]{0:T(512)S(1)}, u32[]{:S(2)}) copy-start(f32[512]{0:T(512)S(1)} %broadcast_multiply_fusion.1) | copy-start | bytes 6148
  188.0 155.0 %copy-start.33 = (f32[512,768]{1,0:T(8,128)}, f32[512,768]{1,0:T(8,128)S(1)}, u32[]{:S(2)}) copy-start(f32[512,768]{1,0:T(8,128)S(1)} %get-tuple-element.543) | copy-start | bytes 4718596
  188.0 161.3 %copy-start.83 = (f32[512]{0:T(512)}, f32[512]{0:T(512)S(1)}, u32[]{:S(2)}) copy-start(f32[512]{0:T(512)S(1)} %broadcast_multiply_fusion.3) | copy-start | bytes 6148
  188.6 160.7 %copy-start.77 = (f32[512]{0:T(512)}, f32[512]{0:T(512)S(1)}, u32[]{:S(2)}) copy-start(f32[512]{0:T(512)S(1)} %fusion.158) | copy-start | bytes 6148
  188.7 160.7 %copy-start.94 = (f32[512]{0:T(512)}, f32[512]{0:T(512)S(1)}, u32[]{:S(2)}) copy-start(f32[512]{0:T(512)S(1)} %fusion.156) | copy-start | bytes 6148
  234.8 7.9 copy-start.104
  234.8 7.9 copy-start.108
  242.7 56.7 %copy-start.110 = (f32[768]{0:T(1024)S(1)}, f32[768]{0:T(1024)}, u32[]{:S(2)}) copy-start(f32[768]{0:T(1024)} %param.30) | copy-start | bytes 9220
  352.2 8.2 copy-start.8
  352.3 26.5 %copy-start.79 = (f32[512]{0:T(512)}, f32[512]{0:T(512)S(1)}, u32[]{:S(2)}) copy-start(f32[512]{0:T(512)S(1)} %negate_multiply_fusion.2) | copy-start | bytes 6148
  356.1 15.9 %all-to-all-start.2 = ((bf16[512,2,384]{2,0,1:T(8,128)(2,1)}), bf16[512,2,384]{2,0,1:T(8,128)(2,1)}, u32[]{:S(2)}, u32[]{:S(2)}) async-start(bf16[512,2,384]{2,0,1:T(8,128)(2,1)} %bitcast.290), calls=%async_computation.2 | async-start | bytes 1572864 | tf_op jit(solution)/shard_map/all_to_all | solution.py:172
  363.1 18.5 %copy-start.3 = (bf16[2,512,6,64]{1,3,2,0:T(8,128)(2,1)S(1)}, bf16[2,512,6,64]{1,3,2,0:T(8,128)(2,1)}, u32[]{:S(2)}) copy-start(bf16[2,512,6,64]{1,3,2,0:T(8,128)(2,1)} %copy-done.2) | copy-start | bytes 2359300
  363.1 18.5 %copy-start.7 = (bf16[2,512,6,64]{1,3,2,0:T(8,128)(2,1)S(1)}, bf16[2,512,6,64]{1,3,2,0:T(8,128)(2,1)}, u32[]{:S(2)}) copy-start(bf16[2,512,6,64]{1,3,2,0:T(8,128)(2,1)} %copy-done.6) | copy-start | bytes 2359300
  363.1 18.5 %copy-start.65 = (f32[2,6,512]{2,1,0:T(8,128)S(1)}, f32[2,6,512]{2,1,0:T(8,128)}, u32[]{:S(2)}) copy-start(f32[2,6,512]{2,1,0:T(8,128)} %copy-done.64) | copy-start | bytes 73732
  363.1 18.5 %copy-start.69 = (s32[2,512]{1,0:T(2,128)S(1)}, s32[2,512]{1,0:T(2,128)}, u32[]{:S(2)}) copy-start(s32[2,512]{1,0:T(2,128)} %copy-done.68) | copy-start | bytes 12292
  372.0 32.6 %all-to-all-start.3 = ((bf16[512,2,384]{2,0,1:T(8,128)(2,1)}), bf16[512,2,384]{2,0,1:T(8,128)(2,1)}, u32[]{:S(2)}, u32[]{:S(2)}) async-start(bf16[512,2,384]{2,0,1:T(8,128)(2,1)} %bitcast.289), calls=%async_computation.4 | async-start | bytes 1572864 | tf_op jit(solution)/shard_map/all_to_all | solution.py:172
  376.3 202.8 %all-reduce.4.cloned.1.call-start = ((), (), s32[]{:S(2)}) async-start(), calls=%async_computation.20 | async-start | bytes 9437184
  436.2 15.2 %copy-start.52 = (bf16[1,1024,384]{2,1,0:T(8,128)(2,1)}, bf16[1,1024,384]{2,1,0:T(8,128)(2,1)S(1)}, u32[]{:S(2)}) copy-start(bf16[1,1024,384]{2,1,0:T(8,128)(2,1)S(1)} %copy.141) | copy-start | bytes 2359300
  462.1 144.8 %reduce-scatter.6.cloned.1.call-start = ((), (), s32[]{:S(2)}) async-start(), calls=%async_computation.13 | async-start | bytes 2359296 | tf_op jit(solution)/shard_map/reduce_scatter | solution.py:187
  468.6 166.8 %reduce-scatter.8.cloned.1.call-start = ((), (), s32[]{:S(2)}) async-start(), calls=%async_computation.14 | async-start | bytes 2359296 | tf_op jit(solution)/shard_map/reduce_scatter | solution.py:187
  474.1 266.6 %reduce-scatter.10.cloned.1.call-start = ((), (), s32[]{:S(2)}) async-start(), calls=%async_computation.17 | async-start | bytes 2433024 | tf_op jit(solution)/shard_map/reduce_scatter | solution.py:85
  478.8 403.6 %reduce-scatter.14.cloned.1.call-start = ((), (), s32[]{:S(2)}) async-start(), calls=%async_computation.19 | async-start | bytes 9732096 | tf_op jit(solution)/shard_map/reduce_scatter | solution.py:87
  489.3 534.6 %reduce-scatter.12.cloned.1.call-start = ((), (), s32[]{:S(2)}) async-start(), calls=%async_computation.18 | async-start | bytes 9732096 | tf_op jit(solution)/shard_map/reduce_scatter | solution.py:86
  504.2 102.7 %copy-start.11 = (f32[512,768]{1,0:T(8,128)S(1)}, f32[512,768]{1,0:T(8,128)}, u32[]{:S(2)}) copy-start(f32[512,768]{1,0:T(8,128)} %copy-done.10) | copy-start | bytes 4718596
  504.2 102.7 %copy-start.82 = (f32[512]{0:T(512)S(1)}, f32[512]{0:T(512)}, u32[]{:S(2)}) copy-start(f32[512]{0:T(512)} %copy-done.81) | copy-start | bytes 6148
  510.1 125.2 %copy-start.9 = (f32[512,768]{1,0:T(8,128)S(1)}, f32[512,768]{1,0:T(8,128)}, u32[]{:S(2)}) copy-start(f32[512,768]{1,0:T(8,128)} %copy-done.8) | copy-start | bytes 4718596
  510.1 125.2 %copy-start.80 = (f32[512]{0:T(512)S(1)}, f32[512]{0:T(512)}, u32[]{:S(2)}) copy-start(f32[512]{0:T(512)} %copy-done.79) | copy-start | bytes 6148
  609.4 27.3 %copy-start.32 = (f32[1,512,768]{2,1,0:T(8,128)S(1)}, f32[1,512,768]{2,1,0:T(8,128)}, u32[]{:S(2)}) copy-start(f32[1,512,768]{2,1,0:T(8,128)} %add_bitcast_fusion.2) | copy-start | bytes 4718596
  (96 other events, 310.3 us)
Sparse Core Ops, SparseCore 0:
  10.1 29.8 all-gather.18
  42.4 40.4 all-gather.8
  85.0 25.8 all-gather.16
  113.7 55.4 all-gather.10
  171.9 62.8 all-gather.12
  237.6 61.8 all-gather.14
  462.2 116.8 all-reduce.3
  581.4 25.4 reduce-scatter.5
  609.1 26.1 reduce-scatter.7
  641.1 99.6 reduce-scatter.9
  747.2 135.1 reduce-scatter.13
  888.7 135.1 reduce-scatter.11
where the time goes:
time: 1040 us; the launch traced here: 1030 us
  waiting for transfers between devices  641 us (62%)
  matrix products  187 us (18%)
  local copies, waits for them, and re-layouts  78.7 us (8%)
  other arithmetic  46.2 us (4%)
  blocking collectives  42.3 us (4%)
  starting transfers between devices  17.2 us (2%)
  between operations  16.5 us (2%)
    reduce_scatter x1, waiting for transfers between devices, reduce_tokens(): lax.psum_scatter(token_terms[2], ('dp', 'head'), scatter_dimension=1, til...  142 us
    reduce_scatter x1, waiting for transfers between devices, reduce_tokens(): lax.psum_scatter(token_terms[1], ('dp', 'head'), scatter_dimension=1, til...  142 us
    reduce_scatter x1, waiting for transfers between devices, reduce_tokens(): lax.psum_scatter(token_terms[0], ('dp', 'head'), scatter_dimension=1, til...  102 us
    reduce_scatter x2, waiting for transfers between devices, on_device(): lax.psum_scatter(jnp.einsum('ctf,cdf->td', grad_proj, head_full, preferre...  52 us
    all_gather x2, waiting for transfers between devices, on_device(): x_group = lax.all_gather(x_local, 'head', axis=0, tiled=True)  48.8 us
    all_gather x1, waiting for transfers between devices, fetch_weights(): lax.all_gather(w_in, ('dp', 'head'), axis=1, tiled=True)  46.1 us
    all_gather x1, waiting for transfers between devices, fetch_weights(): head_full = lax.all_gather(w_qkv, 'dp', axis=1, tiled=True)  42.8 us
    psum x1, blocking collectives, on_device(): lax.psum((small_total[0], small_total[1], small_total[2], small_total[3],...  42.3 us
  transfers between devices with their start and end apart: 16, of which 13 were waited for; matrix products, arithmetic and copies ran while one was open for 18% of the time, Pallas kernels for 0%

commit v1 on v0

--- a/solution.py
+++ b/solution.py
@@ -67,7 +67,16 @@
 
 
 def fetch_weights(w_qkv, w_out, w_in, w_back):
-    head_full = lax.all_gather(w_qkv, "dp", axis=1, tiled=True)
+    ways = lax.axis_size("dp")
+    up = [(d, (d + 1) % ways) for d in range(ways)]
+    down = [(d, (d - 1) % ways) for d in range(ways)]
+    earlier, later = ([w_qkv], [w_qkv])
+    for _ in range(ways // 2):
+        earlier.append(lax.ppermute(earlier[-1], "dp", up))
+    for _ in range((ways - 1) // 2):
+        later.append(lax.ppermute(later[-1], "dp", down))
+    line = jnp.concatenate([*earlier[::-1], *later[1:]], axis=1)
+    head_full = jnp.roll(line, (lax.axis_index("dp") - ways // 2) * w_qkv.shape[1], axis=1)
     out_full, in_full, back_full = (
         lax.all_gather(w_out, ("dp", "head"), axis=1, tiled=True),
         lax.all_gather(w_in, ("dp", "head"), axis=1, tiled=True),

time: 1040 us -> 992 us (0.954)
  waiting for transfers between devices: 641 us -> 556 us
  starting transfers between devices: 17.2 us -> 49.3 us
    all_gather x2, waiting for transfers between devices: 48.8 us -> 0.02 us  [on_device(): x_group = lax.all_gather(x_local, 'head', axis=0, tiled=True)]
    all_gather x1 -> x0, waiting for transfers between devices: 42.8 us -> none  [fetch_weights(): head_full = lax.all_gather(w_qkv, 'dp', axis=1, tiled=True)]
    ppermute x0 -> x15, waiting for transfers between devices: none -> 35.7 us  [the longest x8 35.4 us: fetch_weights(): earlier.append(lax.ppermute(earlier[-1], 'dp', up))]
    ppermute x0 -> x15, starting transfers between devices: none -> 32.1 us  [the longest x7 30.9 us: fetch_weights(): later.append(lax.ppermute(later[-1], 'dp', down))]
    all_gather x1, waiting for transfers between devices: 46.1 us -> 20 us  [fetch_weights(): lax.all_gather(w_in, ('dp', 'head'), axis=1, tiled=True)]
    unnamed x13 -> x12, waiting for transfers between devices: 28.1 us -> 27.8 us
  transfers between devices with their start and end apart: 16 -> 30, of which waited for: 13 -> 19; matrix products, arithmetic and copies ran while one was open for 18% -> 20% of each run, Pallas kernels for 0% -> 0%
where the time goes in v1:
time: 992 us; the launch traced here: 987 us
  waiting for transfers between devices  556 us (56%)
  matrix products  188 us (19%)
  local copies, waits for them, and re-layouts  87.9 us (9%)
  starting transfers between devices  49.3 us (5%)
  other arithmetic  46.5 us (5%)
  blocking collectives  42.1 us (4%)
  between operations  16.3 us (2%)
    reduce_scatter x1, waiting for transfers between devices, reduce_tokens(): lax.psum_scatter(token_terms[1], ('dp', 'head'), scatter_dimension=1, til...  142 us
    reduce_scatter x1, waiting for transfers between devices, reduce_tokens(): lax.psum_scatter(token_terms[2], ('dp', 'head'), scatter_dimension=1, til...  142 us
    reduce_scatter x1, waiting for transfers between devices, reduce_tokens(): lax.psum_scatter(token_terms[0], ('dp', 'head'), scatter_dimension=1, til...  102 us
    reduce_scatter x2, waiting for transfers between devices, on_device(): lax.psum_scatter(jnp.einsum('ctf,cdf->td', grad_proj, head_full, preferre...  52.1 us
    psum x1, blocking collectives, on_device(): lax.psum((small_total[0], small_total[1], small_total[2], small_total[3],...  42.1 us
    dot_general x2, matrix products, on_device(): jnp.dot(hidden_low, in_full, preferred_element_type=jnp.float32) + in_bias  40.7 us
    ppermute x8, waiting for transfers between devices, fetch_weights(): earlier.append(lax.ppermute(earlier[-1], 'dp', up))  35.4 us
    ppermute x7, starting transfers between devices, fetch_weights(): later.append(lax.ppermute(later[-1], 'dp', down))  30.9 us
  transfers between devices with their start and end apart: 30, of which 19 were waited for; matrix products, arithmetic and copies ran while one was open for 20% of the time, Pallas kernels for 0%

profile of v1, /device:TPU:0, one launch (start us, length us, event | category | flops | bytes accessed | tf_op | source)
XLA Modules:
  0.0 987.4 jit_solution(3943101618477350734)
XLA Ops:
  12.8 5.0 collective-permute-start.8
  17.8 4.4 collective-permute-done
  22.3 4.5 collective-permute-start.9
  26.8 4.4 collective-permute-done.1
  31.5 4.2 collective-permute-start.10
  35.7 4.4 collective-permute-done.2
  40.2 4.5 collective-permute-start.11
  44.7 4.4 collective-permute-done.3
  53.6 4.4 collective-permute-done.4
  58.1 4.5 collective-permute-start.13
  62.6 4.4 collective-permute-done.5
  69.3 4.4 collective-permute-start.14
  78.7 6.6 collective-permute-done.7
  85.3 6.1 concatenate.7
  99.1 4.0 convolution_bitcast_fusion
  111.0 4.0 squeeze.84
  118.1 4.8 fusion.150
  123.9 11.0 %while.52 = (s32[]{:T(128)}, bf16[2,512,6,64]{1,3,2,0:T(8,128)(2,1)}, f32[2,6,512]{2,1,0:T(8,128)S(1)}, bf16[2,512,6,64]{1,3,2,0:T(8,128)(2,1)}, s32[2,512]{1,0:...) while((s32[]{:T(128)}, ...), condition=%wide.region_3.5_spmd, body=%wide.region_0.4_spmd.sunk | while | flops 421983232 | bytes 24768632 | solution.py:147
  134.9 4.3 all-to-all-start
  144.9 11.0 %while.53 = (s32[]{:T(128)}, bf16[2,512,6,64]{1,3,2,0:T(8,128)(2,1)}, f32[2,6,512]{2,1,0:T(8,128)S(1)}, bf16[2,512,6,64]{1,3,2,0:T(8,128)(2,1)S(1)}, s32[2,512]{...) while((s32[]{:T(128)}, ...), condition=%wide.region_11.13_spmd, body=%wide.region_8.12_spmd.sunk | while | flops 421983232 | bytes 21622876 | solution.py:147
  163.3 5.1 all-to-all-done.1
  172.6 20.0 %all-gather.10.cloned.1.call-done = bf16[768,3072]{0,1:T(8,128)(2,1)} async-done(((bf16[768,96]{0,1:T(8,128)(2,1)}), bf16[768,3072]{0,1:T(8,128)(2,1)}) %all-gather.10.cloned.1.call-update) | async-done | bytes 4718608 | tf_op jit(solution)/shard_map/all_gather | solution.py:82
  192.7 5.2 fusion.166
  200.6 35.5 %multiply_convert_fusion.3 = (bf16[512,3072]{1,0:T(8,128)(2,1)}, f32[512,3072]{1,0:T(8,128)}, bf16[512,3072]{1,0:T(8,128)(2,1)}, f32[512,3072]{1,0:T(8,128)}, f32[512,3072]{1,0:T(8,128)}) fusion(f32[3072]{0:T(1024)S(1)} %copy-done.115, f32[512,3072]{1,0:T(8,128)S(1)} %fusion.166, bf16[768,3072]{0,1:T(8,128)(2,1)S(1)} %copy-done.111, ...), kind=kOutput, calls=%fused_computation.153 | convolution fusion | flops 2625503232 | bytes 37771264 | tf_op jit(solution)/shard_map/dot_general | solution.py:154
  236.1 21.3 %all-gather.12.cloned.1.call-done = bf16[3072,768]{0,1:T(8,128)(2,1)} async-done(((bf16[3072,24]{0,1:T(8,128)(2,1)}), bf16[3072,768]{0,1:T(8,128)(2,1)}) %all-gather.12.cloned.1.call-update) | async-done | bytes 4718608 | tf_op jit(solution)/shard_map/all_gather | solution.py:83
  257.4 6.2 fusion.184
  277.4 17.3 %convert_reduce_fusion.1 = (f32[3072]{0:T(1024)}, bf16[512,3072]{1,0:T(8,128)(2,1)}, f32[3072]{0:T(1024)}, bf16[512,3072]{1,0:T(8,128)(2,1)}) fusion(f32[512,3072]{1,0:T(8,128)} %get-tuple-element.506, f32[512,3072]{1,0:T(8,128)} %get-tuple-element.547, f32[3072]{0:T(1024)S(1)} %copy-done.115, f32[512,3072]{1,0:T(8,128)S(1)} %fusion.185, ...), kind=kOutput, calls=%fused_computation.137 | convolution fusion | flops 2469390336 | bytes 43290624 | tf_op jit(solution)/shard_map/td,fd->tf/dot_general | solution.py:165
  294.7 6.5 add_add_fusion.6
  301.2 6.3 multiply_reduce_fusion.3
  312.9 4.3 all-to-all-start.2
  319.9 8.8 all-to-all-done.2
  328.7 4.3 all-to-all-start.3
  338.3 22.9 %while.54 = (s32[]{:T(128)}, bf16[2,512,6,64]{1,3,2,0:T(8,128)(2,1)}, bf16[2,512,6,64]{1,3,2,0:T(8,128)(2,1)}, bf16[2,512,6,64]{1,3,2,0:T(8,128)(2,1)}, bf16[2,5...) while((s32[]{:T(128)}, ...), condition=%wide.region_22.24_spmd, body=%wide.region_20.23_spmd.sunk | while | flops 1031468032 | bytes 68001024 | solution.py:182
  366.6 23.5 %while.55 = (s32[]{:T(128)}, bf16[2,512,6,64]{1,3,2,0:T(8,128)(2,1)}, bf16[2,512,6,64]{1,3,2,0:T(8,128)(2,1)}, bf16[2,512,6,64]{1,3,2,0:T(8,128)(2,1)}, bf16[2,5...) while((s32[]{:T(128)}, ...), condition=%wide.region_30.32_spmd, body=%wide.region_28.31_spmd.sunk | while | flops 1031468032 | bytes 68001024 | solution.py:182
  408.2 4.1 fusion.145
  420.3 4.8 bitcast_convert_fusion.1
  425.1 5.4 bitcast_convert_fusion
  435.1 4.8 fusion.187
  440.0 5.5 convolution_add_fusion
  446.9 4.8 fusion.168
  451.8 5.4 convolution_add_fusion.1
  467.8 42.1 %all-reduce.1 = (f32[2,768]{1,0:T(2,128)}, f32[768]{0:T(1024)}, f32[3072]{0:T(1024)}, f32[768]{0:T(1024)}, f32[2,768]{1,0:T(2,128)}, /*index=5*/f32[2,768]{1,0:T(2,128)}) all-reduce(f32[2,768]{1,0:T(2,128)S(1)} %fusion.156, f32[768]{0:T(1024)S(1)} %add.330, f32[3072]{0:T(1024)S(1)} %add.332, ...), channel_id=1, replica_groups=mesh['dp'=16,'head'=2] {'dp','head'}, use_global_device_ids=true, to_apply=%region_38.40 | all-reduce | flops 9216 | bytes 73728 | tf_op jit(solution)/shard_map/psum | solution.py:228
  509.9 25.8 %all-reduce.4.cloned.1.call-done = f32[3,768,384]{2,0,1:T(4,128)} async-done(((f32[3,768,384]{2,0,1:T(4,128)}), f32[3,768,384]{2,0,1:T(4,128)}) %all-reduce.4.cloned.1.call-update) | async-done | bytes 3538960
  537.4 26.2 %reduce-scatter.6.cloned.1.call-done = bf16[512,768]{1,0:T(8,128)(2,1)} async-done(((bf16[1024,768]{1,0:T(8,128)(2,1)}), bf16[512,768]{1,0:T(8,128)(2,1)}) %reduce-scatter.6.cloned.1.call-update) | async-done | bytes 786448 | tf_op jit(solution)/shard_map/reduce_scatter | solution.py:196
  566.1 25.9 %reduce-scatter.8.cloned.1.call-done = bf16[512,768]{1,0:T(8,128)(2,1)} async-done(((bf16[1024,768]{1,0:T(8,128)(2,1)}), bf16[512,768]{1,0:T(8,128)(2,1)}) %reduce-scatter.8.cloned.1.call-update) | async-done | bytes 786448 | tf_op jit(solution)/shard_map/reduce_scatter | solution.py:196
  595.3 102.2 %reduce-scatter.10.cloned.1.call-done = f32[768,24]{0,1:T(8,128)} async-done(((f32[768,768]{0,1:T(8,128)}), f32[768,24]{0,1:T(8,128)}) %reduce-scatter.10.cloned.1.call-update) | async-done | bytes 73744 | tf_op jit(solution)/shard_map/reduce_scatter | solution.py:94
  697.5 141.6 %reduce-scatter.14.cloned.1.call-done = f32[3072,24]{0,1:T(8,128)} async-done(((f32[3072,768]{0,1:T(8,128)}), f32[3072,24]{0,1:T(8,128)}) %reduce-scatter.14.cloned.1.call-update) | async-done | bytes 294928 | tf_op jit(solution)/shard_map/reduce_scatter | solution.py:96
  839.1 141.6 %reduce-scatter.12.cloned.1.call-done = f32[768,96]{0,1:T(8,128)} async-done(((f32[768,3072]{0,1:T(8,128)}), f32[768,96]{0,1:T(8,128)}) %reduce-scatter.12.cloned.1.call-update) | async-done | bytes 294928 | tf_op jit(solution)/shard_map/reduce_scatter | solution.py:95
  (492 shorter events, 205.5 us)
Async XLA Ops:
  7.2 59.8 %copy-start.106 = (s32[2,2,512]{2,1,0:T(2,128)S(1)}, s32[2,2,512]{2,1,0:T(2,128)}, u32[]{:S(2)}) copy-start(s32[2,2,512]{2,1,0:T(2,128)} %param.24) | copy-start | bytes 24580
  7.2 86.0 %all-gather.14.cloned.1.call-start = ((), (), s32[]{:S(2)}) async-start(), calls=%async_computation.14 | async-start | bytes 2359296 | tf_op jit(solution)/shard_map/all_gather | solution.py:139
  9.9 89.2 %all-gather.16.cloned.1.call-start = ((), (), s32[]{:S(2)}) async-start(), calls=%async_computation.15 | async-start | bytes 2359296 | tf_op jit(solution)/shard_map/all_gather | solution.py:139
  10.6 148.9 %all-gather.8.cloned.1.call-start = ((), (), s32[]{:S(2)}) async-start(), calls=%async_computation.9 | async-start | bytes 1216512 | tf_op jit(solution)/shard_map/all_gather | solution.py:81
  11.4 181.3 %all-gather.10.cloned.1.call-start = ((), (), s32[]{:S(2)}) async-start(), calls=%async_computation.10 | async-start | bytes 4866048 | tf_op jit(solution)/shard_map/all_gather | solution.py:82
  11.9 245.4 %all-gather.12.cloned.1.call-start = ((), (), s32[]{:S(2)}) async-start(), calls=%async_computation.11 | async-start | bytes 4866048 | tf_op jit(solution)/shard_map/all_gather | solution.py:83
  12.2 10.0 %collective-permute-start = (bf16[3,48,384]{1,2,0:T(8,128)(2,1)S(1)}, bf16[3,48,384]{1,2,0:T(8,128)(2,1)S(1)}, u32[]{:S(2)}, u32[]{:S(2)}) collective-permute-start(bf16[3,48,384]{1,2,0:T(8,128)(2,1)S(1)} %copy.144), channel_id=1, source_target_pairs={{0,2},{2,4},{4,6},{6,8},{8,10},{10,12},{12,14},{14,16},{16,18},{18... | collective-permute-start | bytes 331784 | tf_op jit(solution)/shard_map/ppermute | solution.py:75
  12.8 9.5 collective-permute-start.8
  22.3 8.9 collective-permute-start.1
  22.3 9.3 collective-permute-start.9
  31.2 8.9 collective-permute-start.2
  31.5 8.6 collective-permute-start.10
  40.2 8.9 collective-permute-start.3
  40.2 8.9 collective-permute-start.11
  49.1 8.9 collective-permute-start.4
  49.8 28.1 %copy-start.68 = (bf16[3,48,384]{1,2,0:T(8,128)(2,1)}, bf16[3,48,384]{1,2,0:T(8,128)(2,1)S(1)}, u32[]{:S(2)}) copy-start(bf16[3,48,384]{1,2,0:T(8,128)(2,1)S(1)} %collective-permute-done.11) | copy-start | bytes 331780
  49.8 8.3 collective-permute-start.12
  58.0 19.9 %copy-start.69 = (bf16[3,48,384]{1,2,0:T(8,128)(2,1)}, bf16[3,48,384]{1,2,0:T(8,128)(2,1)S(1)}, u32[]{:S(2)}) copy-start(bf16[3,48,384]{1,2,0:T(8,128)(2,1)S(1)} %collective-permute-done.4) | copy-start | bytes 331780
  58.1 8.9 collective-permute-start.5
  58.1 19.9 %copy-start.70 = (bf16[3,48,384]{1,2,0:T(8,128)(2,1)}, bf16[3,48,384]{1,2,0:T(8,128)(2,1)S(1)}, u32[]{:S(2)}) copy-start(bf16[3,48,384]{1,2,0:T(8,128)(2,1)S(1)} %collective-permute-done.12) | copy-start | bytes 331780
  58.1 11.2 %collective-permute-start.13 = (bf16[3,48,384]{1,2,0:T(8,128)(2,1)S(1)}, bf16[3,48,384]{1,2,0:T(8,128)(2,1)S(1)}, u32[]{:S(2)}, u32[]{:S(2)}) collective-permute-start(bf16[3,48,384]{1,2,0:T(8,128)(2,1)S(1)} %collective-permute-done.12), channel_id=1, source_target_pairs={{0,30},{2,0},{4,2},{6,4},{8,6},{10,8},{12,10},{14,12},{16,14},{18,... | collective-permute-start | bytes 331784 | tf_op jit(solution)/shard_map/ppermute | solution.py:77
  67.0 8.9 collective-permute-start.6
  69.3 8.6 collective-permute-start.14
  75.9 9.3 collective-permute-start.7
  134.9 21.0 %all-to-all-start = ((bf16[2,512,384]{1,2,0:T(8,128)(2,1)}), bf16[2,512,384]{1,2,0:T(8,128)(2,1)}, u32[]{:S(2)}, u32[]{:S(2)}) async-start(bf16[2,512,384]{1,2,0:T(8,128)(2,1)} %bitcast.43), calls=%async_computation | async-start | bytes 1572864 | tf_op jit(solution)/shard_map/all_to_all | solution.py:149
  155.9 12.4 %all-to-all-start.1 = ((bf16[2,512,384]{1,2,0:T(8,128)(2,1)}), bf16[2,512,384]{1,2,0:T(8,128)(2,1)S(1)}, u32[]{:S(2)}, u32[]{:S(2)}) async-start(bf16[2,512,384]{1,2,0:T(8,128)(2,1)} %bitcast.52), calls=%async_computation.1 | async-start | bytes 1572864 | tf_op jit(solution)/shard_map/all_to_all | solution.py:149
  163.3 144.3 %copy-start.93 = (f32[512]{0:T(512)}, f32[512]{0:T(512)S(1)}, u32[]{:S(2)}) copy-start(f32[512]{0:T(512)S(1)} %broadcast_multiply_fusion.3) | copy-start | bytes 6148
  169.3 23.4 %copy-start.79 = (f32[768]{0:T(1024)S(1)}, f32[768]{0:T(1024)}, u32[]{:S(2)}) copy-start(f32[768]{0:T(1024)} %get-tuple-element.555) | copy-start | bytes 9220
  169.3 23.4 %copy-start.82 = (f32[768]{0:T(1024)S(1)}, f32[768]{0:T(1024)}, u32[]{:S(2)}) copy-start(f32[768]{0:T(1024)} %get-tuple-element.408) | copy-start | bytes 9220
  171.9 135.6 %copy-start.14 = (f32[512,768]{1,0:T(8,128)}, f32[512,768]{1,0:T(8,128)S(1)}, u32[]{:S(2)}) copy-start(f32[512,768]{1,0:T(8,128)S(1)} %get-tuple-element.546) | copy-start | bytes 4718596
  172.0 135.6 %copy-start.84 = (f32[512]{0:T(512)}, f32[512]{0:T(512)S(1)}, u32[]{:S(2)}) copy-start(f32[512]{0:T(512)S(1)} %broadcast_multiply_fusion.1) | copy-start | bytes 6148
  172.6 135.0 %copy-start.104 = (f32[512]{0:T(512)}, f32[512]{0:T(512)S(1)}, u32[]{:S(2)}) copy-start(f32[512]{0:T(512)S(1)} %fusion.157) | copy-start | bytes 6148
  172.6 135.0 %copy-start.87 = (f32[512]{0:T(512)}, f32[512]{0:T(512)S(1)}, u32[]{:S(2)}) copy-start(f32[512]{0:T(512)S(1)} %fusion.159) | copy-start | bytes 6148
  200.6 56.8 %copy-start.117 = (f32[768]{0:T(1024)S(1)}, f32[768]{0:T(1024)}, u32[]{:S(2)}) copy-start(f32[768]{0:T(1024)} %param.32) | copy-start | bytes 9220
  309.2 26.3 %copy-start.89 = (f32[512]{0:T(512)}, f32[512]{0:T(512)S(1)}, u32[]{:S(2)}) copy-start(f32[512]{0:T(512)S(1)} %negate_multiply_fusion.2) | copy-start | bytes 6148
  312.9 15.9 %all-to-all-start.2 = ((bf16[512,2,384]{2,0,1:T(8,128)(2,1)}), bf16[512,2,384]{2,0,1:T(8,128)(2,1)}, u32[]{:S(2)}, u32[]{:S(2)}) async-start(bf16[512,2,384]{2,0,1:T(8,128)(2,1)} %bitcast.290), calls=%async_computation.2 | async-start | bytes 1572864 | tf_op jit(solution)/shard_map/all_to_all | solution.py:181
  328.7 32.5 %all-to-all-start.3 = ((bf16[512,2,384]{2,0,1:T(8,128)(2,1)}), bf16[512,2,384]{2,0,1:T(8,128)(2,1)}, u32[]{:S(2)}, u32[]{:S(2)}) async-start(bf16[512,2,384]{2,0,1:T(8,128)(2,1)} %bitcast.289), calls=%async_computation.4 | async-start | bytes 1572864 | tf_op jit(solution)/shard_map/all_to_all | solution.py:181
  333.1 202.6 %all-reduce.4.cloned.1.call-start = ((), (), s32[]{:S(2)}) async-start(), calls=%async_computation.19 | async-start | bytes 9437184
  418.6 144.9 %reduce-scatter.6.cloned.1.call-start = ((), (), s32[]{:S(2)}) async-start(), calls=%async_computation.12 | async-start | bytes 2359296 | tf_op jit(solution)/shard_map/reduce_scatter | solution.py:196
  425.1 166.9 %reduce-scatter.8.cloned.1.call-start = ((), (), s32[]{:S(2)}) async-start(), calls=%async_computation.13 | async-start | bytes 2359296 | tf_op jit(solution)/shard_map/reduce_scatter | solution.py:196
  430.5 267.0 %reduce-scatter.10.cloned.1.call-start = ((), (), s32[]{:S(2)}) async-start(), calls=%async_computation.16 | async-start | bytes 2433024 | tf_op jit(solution)/shard_map/reduce_scatter | solution.py:94
  435.1 404.0 %reduce-scatter.14.cloned.1.call-start = ((), (), s32[]{:S(2)}) async-start(), calls=%async_computation.18 | async-start | bytes 9732096 | tf_op jit(solution)/shard_map/reduce_scatter | solution.py:96
  445.5 535.1 %reduce-scatter.12.cloned.1.call-start = ((), (), s32[]{:S(2)}) async-start(), calls=%async_computation.17 | async-start | bytes 9732096 | tf_op jit(solution)/shard_map/reduce_scatter | solution.py:95
  460.4 103.1 %copy-start.11 = (f32[512,768]{1,0:T(8,128)S(1)}, f32[512,768]{1,0:T(8,128)}, u32[]{:S(2)}) copy-start(f32[512,768]{1,0:T(8,128)} %copy-done.10) | copy-start | bytes 4718596
  460.4 103.1 %copy-start.92 = (f32[512]{0:T(512)S(1)}, f32[512]{0:T(512)}, u32[]{:S(2)}) copy-start(f32[512]{0:T(512)} %copy-done.91) | copy-start | bytes 6148
  466.2 125.8 %copy-start.9 = (f32[512,768]{1,0:T(8,128)S(1)}, f32[512,768]{1,0:T(8,128)}, u32[]{:S(2)}) copy-start(f32[512,768]{1,0:T(8,128)} %copy-done.8) | copy-start | bytes 4718596
  466.2 125.8 %copy-start.90 = (f32[512]{0:T(512)S(1)}, f32[512]{0:T(512)}, u32[]{:S(2)}) copy-start(f32[512]{0:T(512)} %copy-done.89) | copy-start | bytes 6148
  566.1 27.3 %copy-start.32 = (f32[1,512,768]{2,1,0:T(8,128)S(1)}, f32[1,512,768]{2,1,0:T(8,128)}, u32[]{:S(2)}) copy-start(f32[1,512,768]{2,1,0:T(8,128)} %add_bitcast_fusion.2) | copy-start | bytes 4718596
  (115 other events, 536.2 us)
Sparse Core Ops, SparseCore 0:
  10.1 29.8 all-gather.13
  42.2 27.1 all-gather.15
  72.3 54.0 all-gather.7
  129.2 63.3 all-gather.9
  195.4 61.9 all-gather.11
  418.8 116.8 all-reduce.3
  537.9 25.6 reduce-scatter.5
  565.8 26.1 reduce-scatter.7
  597.8 99.6 reduce-scatter.9
  703.8 135.1 reduce-scatter.13
  845.5 135.0 reduce-scatter.11
